TPU v7x, 512 devices: a whole 4x8x8 slice. The times are simulated.
512 devices in a mesh: dp: 32 (over x, y), seq: 16 (over z, core).
Axes of the slice: x: 4, y: 8, z: 8, core: 2. Of those that a mesh axis runs over, the one named last changes fastest.
Arguments:
- residual_stream: bfloat16 [262144, 2048], P(('dp', 'seq')), parts along dimension 0, may hold values from -6 to 6
- octet_readout: bfloat16 [256, 2048], replicated, may hold values from -6 to 6
- downsampling_filter: bfloat16 [32, 256, 96], replicated, may hold values from -0.375 to 0.375
- sharpness_factor: float32 [8], replicated, may hold values from 4 to 20
- widening_filter: bfloat16 [32, 32, 256], replicated, may hold values from -2 to 2
Outputs:
- logits: bfloat16 [262144, 256], P(('dp', 'seq')), parts along dimension 0
There are 32 independent parts, one for each index of `dp`. A program takes and returns all parts, laid end to end along the dimension named above; an argument that names none is the same for every part. Nothing has to cross between parts.
All inputs are finite; a program needn't handle non-finite values.
Results may differ from a plain program's by a relative error of at most 0.0052.
Values may be sent and summed in bfloat16 or wider, within the bound.
A program may use at most 64 MiB of HBM per device.

v0:
```python
import jax
import jax.numpy as jnp
from jax import lax
from jax.sharding import PartitionSpec as P

SHORTEN = 4


def shifted_2(array, axis, by):
    count = lax.axis_size(axis)
    pairs = [(i, i + by) for i in range(count) if 0 <= i + by < count]
    return lax.ppermute(array, axis, pairs)


def passed_along(block, axis, distance):
    devices = range(lax.axis_size(axis))
    route = [((i - distance) % len(devices), i) for i in devices]
    return lax.ppermute(block, axis, route)


def normalize(vectors):
    return vectors * lax.rsqrt(jnp.sum(vectors * vectors, axis=-1, keepdims=True) + 1e-06)


def shorten(shifted, kernel_part, groups):
    byte_rows, model_width = shifted.shape
    windows = shifted.reshape(byte_rows // SHORTEN, SHORTEN, groups, model_width // groups)
    kernel = kernel_part.reshape(groups, SHORTEN, model_width // groups, kernel_part.shape[2])
    return jnp.einsum("jtgc,gtco->jgo", windows, kernel, preferred_element_type=jnp.float32)


def on_device(
    residual_stream, octet_readout, downsampling_filter, sharpness_factor, widening_filter
):
    byte_rows = residual_stream.shape[0]
    model_width = residual_stream.shape[1]
    groups = downsampling_filter.shape[0]
    group_width = model_width // groups
    per_group = downsampling_filter.shape[2] // 3
    attention_number = sharpness_factor.shape[0]
    head_size = groups * per_group // attention_number
    tokens_here = byte_rows // SHORTEN
    rim_rows = SHORTEN - 1
    left_rim = shifted_2(residual_stream[byte_rows - rim_rows :], "seq", 1)
    shifted = jnp.concatenate([left_rim, residual_stream[: byte_rows - rim_rows]], 0)
    mixed_out = shorten(shifted, downsampling_filter, groups)
    queries = normalize(
        mixed_out[:, :, :per_group].reshape(tokens_here, attention_number, head_size)
    ).astype(jnp.bfloat16)
    key_unit = normalize(
        mixed_out[:, :, per_group : 2 * per_group].reshape(tokens_here, attention_number, head_size)
    ).astype(jnp.bfloat16)
    values = (
        mixed_out[:, :, 2 * per_group :]
        .reshape(tokens_here, attention_number, head_size)
        .astype(jnp.bfloat16)
    )
    my_index = lax.axis_index("seq")
    first_token = my_index * tokens_here
    sharpness_vertical = sharpness_factor[:, None, None]
    query_pos = first_token + jnp.arange(tokens_here, dtype=jnp.int32)
    stacked = jnp.stack([key_unit, values], 0)
    gathered = lax.all_gather(stacked, "seq", axis=1, tiled=True)
    all_keys, all_values = (gathered[0], gathered[1])
    similarity_matrix = (
        jnp.einsum("jsg,isg->sji", queries, all_keys, preferred_element_type=jnp.float32)
        * sharpness_vertical
    )
    key_pos = jnp.arange(all_keys.shape[0], dtype=jnp.int32)
    future_masked = key_pos[None, :] <= query_pos[:, None]
    softmax_shares = jnp.where(
        future_masked[None],
        jnp.exp(similarity_matrix - sharpness_vertical),
        jnp.zeros((), jnp.float32),
    )
    denom_sum = jnp.sum(softmax_shares, axis=-1)
    weighted = jnp.einsum(
        "hqk,khd->qhd",
        softmax_shares.astype(jnp.bfloat16),
        all_values,
        preferred_element_type=jnp.float32,
    )
    attended = (weighted / jnp.transpose(denom_sum)[:, :, None]).astype(jnp.bfloat16)
    attended = attended.reshape(tokens_here, groups, per_group)
    upsampled = jnp.einsum(
        "jgc,gcu->jgu", attended, widening_filter, preferred_element_type=jnp.float32
    )
    upsampled = (
        upsampled.reshape(tokens_here, groups, SHORTEN, group_width)
        .transpose(0, 2, 1, 3)
        .reshape(byte_rows, model_width)
    )
    hidden = residual_stream.astype(jnp.float32) + upsampled
    normed = (hidden * lax.rsqrt(jnp.mean(hidden * hidden, axis=-1, keepdims=True) + 1e-05)).astype(
        jnp.bfloat16
    )
    logits = lax.dot_general(
        normed, octet_readout, (((1,), (1,)), ((), ())), preferred_element_type=jnp.float32
    ) * model_width ** (-0.5)
    return logits.astype(jnp.bfloat16)


def solution(mesh):
    in_specs = (P(("dp", "seq"), None), P(), P(), P(), P())
    out_specs = P(("dp", "seq"), None)
    return jax.shard_map(
        on_device, mesh=mesh, in_specs=in_specs, out_specs=out_specs, check_vma=False
    )
```

profile of v0, /device:TPU:1, one launch (start us, length us, event | category | flops | bytes accessed | tf_op | source)
XLA Modules:
  0.0 155.1 jit_solution(6165816291397608881)
XLA Ops:
  6.5 0.0 copy-start
  6.5 0.0 copy-start.2
  6.5 0.0 all-gather.2.cloned.1.call-start
  6.5 0.9 slice.22
  7.5 5.5 %collective-permute-start = (bf16[3,2048]{1,0:T(4,128)(2,1)S(1)}, bf16[3,2048]{1,0:T(4,128)(2,1)S(1)}, u32[]{:S(2)}, u32[]{:S(2)}) collective-permute-start(bf16[3,2048]{1,0:T(4,128)(2,1)S(1)} %slice.22), channel_id=1, source_target_pairs={{0,1},{1,2},{2,3},{3,4},{4,5},{5,6},{6,7},{7,8},{8,9},{9,10},{10,1... | collective-permute-start | bytes 36872 | tf_op jit(solution)/shard_map/ppermute | solution.py:12
  13.0 3.9 %copy.12 = bf16[32,256,96]{2,1,0:T(8,128)(2,1)} copy(bf16[32,256,96]{1,2,0:T(8,128)(2,1)} %param.7) | data formatting | bytes 3145728 | tf_op args[2]
  16.8 0.0 collective-permute-done
  16.8 0.0 copy-done.2
  16.9 1.9 %pad_maximum_fusion = bf16[512,2048]{1,0:T(8,128)(2,1)} fusion(bf16[509,2048]{1,0:T(8,128)(2,1)S(1)} %bitcast.45, bf16[3,2048]{1,0:T(4,128)(2,1)S(1)} %collective-permute-done), kind=kLoop, calls=%fused_computation.17 | loop fusion | flops 4194304 | bytes 4194304 | tf_op jit(solution)/shard_map/concatenate | solution.py:45
  18.8 7.1 %reshape.93 = bf16[128,4,32,64]{3,2,1,0:T(8,128)(2,1)} reshape(bf16[512,2048]{1,0:T(8,128)(2,1)} %pad_maximum_fusion) | data formatting | bytes 4194304 | tf_op jit(solution)/shard_map/reshape | solution.py:27
  25.9 7.8 %fusion.12 = f32[128,32,96]{0,2,1:T(8,128)S(1)} fusion(bf16[32,4,64,96]{3,2,1,0:T(8,128)(2,1)} %bitcast.47, bf16[128,4,32,64]{3,2,1,0:T(8,128)(2,1)} %reshape.93), kind=kOutput, calls=%fused_computation.19 | convolution fusion | flops 201326592 | bytes 5242880 | tf_op jit(solution)/shard_map/jtgc,gtco->jgo/dot_general | solution.py:29
  33.7 0.0 copy-start.5
  33.7 1.1 multiply_reduce_fusion.1
  34.9 0.9 copy.15
  35.7 2.1 %copy.14 = f32[1,128,8,128]{3,1,2,0:T(8,128)} copy(f32[1,128,8,128]{1,3,2,0:T(8,128)} %bitcast.49) | data formatting | bytes 1048576 | tf_op jit(solution)/shard_map/reshape | solution.py:51
  37.8 1.2 multiply_convert_fusion.7
  39.0 1.9 %pad_maximum_fusion.1 = bf16[2,128,8,128]{3,1,2,0:T(8,128)(2,1)} fusion(bf16[1,128,8,128]{3,1,2,0:T(8,128)(2,1)} %copy.15, bf16[1,128,8,128]{3,1,2,0:T(8,128)(2,1)S(1)} %multiply_convert_fusion.7), kind=kLoop, calls=%fused_computation.27 | loop fusion | flops 262144 | bytes 1048576 | tf_op jit(solution)/shard_map/stack | solution.py:62
  40.9 0.0 all-gather.2.cloned.1.call-update
  40.9 0.2 iota_compare_fusion
  41.2 2.0 %copy.16 = f32[128,8,128]{2,0,1:T(8,128)} copy(f32[128,8,128]{0,2,1:T(8,128)} %bitcast.48) | data formatting | bytes 1048576 | tf_op jit(solution)/shard_map/reshape | solution.py:48
  43.2 60.8 %all-gather.2.cloned.1.call-done = bf16[2,2048,8,128]{3,1,2,0:T(8,128)(2,1)} async-done(((bf16[2,128,8,128]{3,1,2,0:T(8,128)(2,1)}), bf16[2,2048,8,128]{3,1,2,0:T(8,128)(2,1)}) %all-gather.2.cloned.1.call-update) | async-done | bytes 8388624 | tf_op jit(solution)/shard_map/all_gather | solution.py:63
  104.0 0.0 copy-done.5
  104.0 0.0 copy-start.4
  104.0 8.3 %fusion = (f32[8,128]{1,0:T(8,128)S(1)}, f32[8,128,2048]{2,1,0:T(8,128)}) fusion(f32[8]{0:T(128)S(1)} %copy-done.5, pred[128,2048]{1,0:T(8,128)(4,1)S(1)} %iota_compare_fusion, bf16[2,2048,8,128]{3,1,2,0:T(8,128)(2,1)} %all-gather.2.cloned.1.call-done, f32[128,8,128]{2,0,1:T(8,128)} %copy.16, f32[128,8]{0,1:T(8,128)S(1)} %add_rsqrt_fusion), kind=kOutput, calls=%fused_computation.1 | convolution fusion | flops 545520640 | bytes 13377568 | tf_op jit(solution)/shard_map/jsg,isg->sji/dot_general | solution.py:66
  112.3 0.0 copy-done.4
  112.3 0.0 copy-start.3
  112.3 5.8 %fusion.23 = bf16[128,8,128]{0,2,1:T(8,128)(2,1)S(1)} fusion(f32[8,128,2048]{2,1,0:T(8,128)} %get-tuple-element.10, f32[8]{0:T(128)S(1)} %copy-done.5, pred[128,2048]{1,0:T(8,128)(4,1)S(1)} %iota_compare_fusion, bf16[2,2048,8,128]{3,1,2,0:T(8,128)(2,1)S(1)} %copy-done.4, f32[128,8]{0,1:T(8,128)S(1)} %bitcast.54), kind=kOutput, calls=%fused_computation.25 | convolution fusion | flops 545521664 | bytes 13111808 | tf_op jit(solution)/shard_map/hqk,khd->qhd/dot_general | solution.py:77
  118.1 0.0 copy-done.3
  118.1 2.7 %convolution_bitcast_fusion = f32[128,32,256]{2,0,1:T(8,128)} fusion(bf16[128,32,32]{0,2,1:T(8,128)(2,1)S(1)} %bitcast.51, bf16[32,32,256]{2,1,0:T(8,128)(2,1)S(1)} %copy-done.3), kind=kOutput, calls=%fused_computation.15 | convolution fusion | flops 67108864 | bytes 4980736 | tf_op jit(solution)/shard_map/jgc,gcu->jgu/dot_general | solution.py:85
  120.8 5.6 %copy.18 = f32[128,32,256]{0,2,1:T(8,128)} copy(f32[128,32,256]{2,0,1:T(8,128)} %convolution_bitcast_fusion) | data formatting | bytes 8388608 | tf_op jit(solution)/shard_map/jgc,gcu->jgu/transpose | solution.py:85
  126.4 9.1 %copy.19 = f32[128,4,32,64]{3,2,1,0:T(8,128)} copy(f32[128,4,32,64]{0,3,1,2:T(8,128)} %bitcast.46) | data formatting | bytes 8388608 | tf_op jit(solution)/shard_map/transpose | solution.py:90
  135.5 7.8 %reshape.99 = f32[512,2048]{1,0:T(8,128)} reshape(f32[128,4,32,64]{3,2,1,0:T(8,128)} %copy.19) | data formatting | bytes 8388608 | tf_op jit(solution)/shard_map/reshape | solution.py:91
  143.3 0.0 copy-start.1
  143.3 3.0 %multiply_reduce_fusion = f32[512]{0:T(512)S(1)} fusion(f32[512,2048]{1,0:T(8,128)} %reshape.99, bf16[512,2048]{1,0:T(8,128)(2,1)S(1)} %copy-done.2), kind=kLoop, calls=%fused_computation.10 | loop fusion | flops 4193792 | bytes 6293504 | tf_op jit(solution)/shard_map/reduce_sum | solution.py:94
  146.3 0.0 copy-done
  146.3 0.5 copy-done.1
  146.8 1.5 fusion.19
  (7 shorter events, 0.1 us)
Async XLA Ops:
  6.5 139.8 %copy-start = (bf16[256,2048]{1,0:T(8,128)(2,1)S(1)}, bf16[256,2048]{1,0:T(8,128)(2,1)}, u32[]{:S(2)}) copy-start(bf16[256,2048]{1,0:T(8,128)(2,1)} %param.6) | copy-start | bytes 3145732
  6.5 10.3 %copy-start.2 = (bf16[512,2048]{1,0:T(8,128)(2,1)S(1)}, bf16[512,2048]{1,0:T(8,128)(2,1)}, u32[]{:S(2)}) copy-start(bf16[512,2048]{1,0:T(8,128)(2,1)} %param.5) | copy-start | bytes 6291460
  6.5 97.4 %all-gather.2.cloned.1.call-start = ((), (), s32[]{:S(2)}) async-start(), calls=%async_computation | async-start | bytes 8912896 | tf_op jit(solution)/shard_map/all_gather | solution.py:63
  7.5 9.4 %collective-permute-start = (bf16[3,2048]{1,0:T(4,128)(2,1)S(1)}, bf16[3,2048]{1,0:T(4,128)(2,1)S(1)}, u32[]{:S(2)}, u32[]{:S(2)}) collective-permute-start(bf16[3,2048]{1,0:T(4,128)(2,1)S(1)} %slice.22), channel_id=1, source_target_pairs={{0,1},{1,2},{2,3},{3,4},{4,5},{5,6},{6,7},{7,8},{8,9},{9,10},{10,1... | collective-permute-start | bytes 36872 | tf_op jit(solution)/shard_map/ppermute | solution.py:12
  33.7 70.3 %copy-start.5 = (f32[8]{0:T(128)S(1)}, f32[8]{0:T(128)}, u32[]{:S(2)}) copy-start(f32[8]{0:T(128)} %param.8) | copy-start | bytes 100
  104.0 8.3 %copy-start.4 = (bf16[2,2048,8,128]{3,1,2,0:T(8,128)(2,1)S(1)}, bf16[2,2048,8,128]{3,1,2,0:T(8,128)(2,1)}, u32[]{:S(2)}) copy-start(bf16[2,2048,8,128]{3,1,2,0:T(8,128)(2,1)} %all-gather.2.cloned.1.call-done) | copy-start | bytes 25165828
  112.3 5.9 %copy-start.3 = (bf16[32,32,256]{2,1,0:T(8,128)(2,1)S(1)}, bf16[32,32,256]{2,1,0:T(8,128)(2,1)}, u32[]{:S(2)}) copy-start(bf16[32,32,256]{2,1,0:T(8,128)(2,1)} %param.9) | copy-start | bytes 1572868
  143.3 3.4 %copy-start.1 = (f32[512,2048]{1,0:T(8,128)S(1)}, f32[512,2048]{1,0:T(8,128)}, u32[]{:S(2)}) copy-start(f32[512,2048]{1,0:T(8,128)} %reshape.99) | copy-start | bytes 12582916
Sparse Core Ops, SparseCore 0:
  41.0 62.9 all-gather.1
where the time goes:
time: 156 us; the launch traced here: 155 us
  waiting for transfers between devices  60.8 us (39%)
  local copies, waits for them, and re-layouts  39.9 us (26%)
  matrix products  26.1 us (17%)
  between operations  13.5 us (9%)
  other arithmetic  9.4 us (6%)
  starting transfers between devices  5.51 us (4%)
    all_gather x1, waiting for transfers between devices, on_device(): gathered = lax.all_gather(stacked, 'seq', axis=1, tiled=True)  60.8 us
    transpose x1, local copies, waits for them, and re-layouts, on_device(): upsampled = upsampled.reshape(tokens_here, groups, SHORTEN, group_width)....  9.14 us
    dot_general x1, matrix products, on_device(): jnp.einsum('jsg,isg->sji', queries, all_keys, preferred_element_type=jnp....  8.29 us
    reshape x1, local copies, waits for them, and re-layouts, on_device(): upsampled = upsampled.reshape(tokens_here, groups, SHORTEN, group_width)....  7.82 us
    dot_general x1, matrix products, shorten(): jnp.einsum('jtgc,gtco->jgo', windows, kernel, preferred_element_type=jnp....  7.76 us
    reshape x1, local copies, waits for them, and re-layouts, shorten(): shifted.reshape(byte_rows // SHORTEN, SHORTEN, groups, model_width // gro...  7.08 us
    dot_general x1, matrix products, on_device(): jnp.einsum('hqk,khd->qhd', softmax_shares.astype(jnp.bfloat16), all_value...  5.85 us
    transpose x1, local copies, waits for them, and re-layouts, on_device(): jnp.einsum('jgc,gcu->jgu', attended, widening_filter, preferred_element_t...  5.56 us
  transfers between devices with their start and end apart: 2, of which 1 were waited for; matrix products, arithmetic and copies ran while one was open for 4% of the time, Pallas kernels for 0%

commit v1 on v0

--- a/solution.py
+++ b/solution.py
@@ -4,6 +4,16 @@
 from jax.sharding import PartitionSpec as P
 
 SHORTEN = 4
+
+
+def rest_the_leaves(shard_in, at_axis):
+    shard_in = jnp.moveaxis(shard_in, 0, at_axis)
+    local_next = shard_in.shape
+    return shard_in.reshape(
+        *local_next[:at_axis],
+        local_next[at_axis] * local_next[at_axis + 1],
+        *local_next[at_axis + 2 :]
+    )
 
 
 def shifted_2(array, axis, by):
@@ -32,6 +42,28 @@
 def on_device(
     residual_stream, octet_readout, downsampling_filter, sharpness_factor, widening_filter
 ):
+
+    def cut_roads(inputs, which_axis, join_dim=1):
+        cores_n = lax.axis_size(which_axis)
+        slots = []
+        for k in tuple(range(cores_n)):
+            slots.append((k, (k + 1) % cores_n))
+        gallery = []
+        for m, p in slots:
+            gallery.append((p, m))
+        arr_now, ready = ([], [])
+        for rr in [*range(cores_n - 1)]:
+            if rr % 2 == 0:
+                then = lax.ppermute(arr_now[-1] if arr_now else inputs, which_axis, slots)
+                arr_now.append(then)
+            else:
+                ready.append(lax.ppermute(ready[-1] if ready else inputs, which_axis, gallery))
+        odd = jnp.stack([*arr_now[::-1], inputs, *ready], 0)
+        seen_now = lax.axis_index(which_axis)
+        x_new = seen_now - len(arr_now)
+        odd = odd[(jnp.arange(cores_n) - x_new) % cores_n]
+        return rest_the_leaves(odd, join_dim)
+
     byte_rows = residual_stream.shape[0]
     model_width = residual_stream.shape[1]
     groups = downsampling_filter.shape[0]
@@ -60,7 +92,7 @@
     sharpness_vertical = sharpness_factor[:, None, None]
     query_pos = first_token + jnp.arange(tokens_here, dtype=jnp.int32)
     stacked = jnp.stack([key_unit, values], 0)
-    gathered = lax.all_gather(stacked, "seq", axis=1, tiled=True)
+    gathered = cut_roads(stacked, "seq")
     all_keys, all_values = (gathered[0], gathered[1])
     similarity_matrix = (
         jnp.einsum("jsg,isg->sji", queries, all_keys, preferred_element_type=jnp.float32)

time: 156 us -> 206 us (1.32)
  the two profiles are of different devices: /device:TPU:1 before, /device:TPU:46 now
where the time goes in v1:
time: 206 us; the launch traced here: 204 us
  local copies, waits for them, and re-layouts  92 us (45%)
  waiting for transfers between devices  59.4 us (29%)
  starting transfers between devices  25.4 us (12%)
  matrix products  21.1 us (10%)
  other arithmetic  6.4 us (3%)
    ppermute x8, waiting for transfers between devices, cut_roads(): then = lax.ppermute(arr_now[-1] if arr_now else inputs, which_axis, slots)  59.2 us
    unnamed x43, local copies, waits for them, and re-layouts  26.2 us
    ppermute x7, starting transfers between devices, cut_roads(): lax.ppermute(ready[-1] if ready else inputs, which_axis, gallery)  20.9 us
    slice x3, local copies, waits for them, and re-layouts, on_device(): all_keys, all_values = (gathered[0], gathered[1])  19.4 us
    transpose x1, local copies, waits for them, and re-layouts, on_device(): upsampled = upsampled.reshape(tokens_here, groups, SHORTEN, group_width)....  9.19 us
    gather x1, local copies, waits for them, and re-layouts, cut_roads(): odd = odd[(jnp.arange(cores_n) - x_new) % cores_n]  8.16 us
    reshape x1, local copies, waits for them, and re-layouts, on_device(): upsampled = upsampled.reshape(tokens_here, groups, SHORTEN, group_width)....  7.97 us
    dot_general x1, matrix products, shorten(): jnp.einsum('jtgc,gtco->jgo', windows, kernel, preferred_element_type=jnp....  7.77 us
  transfers between devices with their start and end apart: 16, of which 9 were waited for; matrix products, arithmetic and copies ran while one was open for 14% of the time, Pallas kernels for 0%

profile of v1, /device:TPU:46, one launch (start us, length us, event | category | flops | bytes accessed | tf_op | source)
XLA Modules:
  0.0 204.5 jit_solution(8699482430355987684)
XLA Ops:
  0.0 0.9 slice.24
  0.9 1.7 collective-permute-start
  2.6 3.9 %copy.11 = bf16[32,256,96]{2,1,0:T(8,128)(2,1)} copy(bf16[32,256,96]{1,2,0:T(8,128)(2,1)} %param.7) | data formatting | bytes 3145728 | tf_op args[2]
  6.5 2.1 %pad_maximum_fusion = bf16[512,2048]{1,0:T(8,128)(2,1)S(1)} fusion(bf16[509,2048]{1,0:T(8,128)(2,1)} %bitcast.74, bf16[3,2048]{1,0:T(4,128)(2,1)S(1)} %collective-permute-done), kind=kLoop, calls=%fused_computation.15 | loop fusion | flops 4194304 | bytes 4194304 | tf_op jit(solution)/shard_map/concatenate | solution.py:77
  8.6 5.3 %reshape.147 = bf16[128,4,32,64]{3,2,1,0:T(8,128)(2,1)} reshape(bf16[512,2048]{1,0:T(8,128)(2,1)S(1)} %pad_maximum_fusion) | data formatting | bytes 4194304 | tf_op jit(solution)/shard_map/reshape | solution.py:37
  13.9 7.8 %fusion.11 = f32[128,32,96]{0,2,1:T(8,128)S(1)} fusion(bf16[32,4,64,96]{3,2,1,0:T(8,128)(2,1)} %bitcast.79, bf16[128,4,32,64]{3,2,1,0:T(8,128)(2,1)} %reshape.147), kind=kOutput, calls=%fused_computation.17 | convolution fusion | flops 201326592 | bytes 5242880 | tf_op jit(solution)/shard_map/jtgc,gtco->jgo/dot_general | solution.py:39
  22.2 2.7 %collective-permute-start.1 = (bf16[2,128,8,128]{1,3,2,0:T(8,128)(2,1)S(1)}, bf16[2,128,8,128]{1,3,2,0:T(8,128)(2,1)S(1)}, u32[]{:S(2)}, u32[]{:S(2)}) collective-permute-start(bf16[2,128,8,128]{1,3,2,0:T(8,128)(2,1)S(1)} %pad_maximum_fusion.1), channel_id=1, source_target_pairs={{0,1},{1,2},{2,3},{3,4},{4,5},{5,6},{6,7},{7,8},{8,9},{9,10},{10,1... | collective-permute-start | bytes 1572872 | tf_op jit(solution)/shard_map/ppermute | solution.py:57
  24.8 12.2 %collective-permute-done.1 = bf16[2,128,8,128]{1,3,2,0:T(8,128)(2,1)S(1)} collective-permute-done((bf16[2,128,8,128]{1,3,2,0:T(8,128)(2,1)S(1)}, bf16[2,128,8,128]{1,3,2,0:T(8,128)(2,1)S(1)}, u32[]{:S(2)}, u32[]{:S(2)}) %collective-permute-start.1) | collective-permute-done | bytes 524320 | tf_op jit(solution)/shard_map/ppermute | solution.py:57
  37.1 3.0 %collective-permute-start.9 = (bf16[2,128,8,128]{1,3,2,0:T(8,128)(2,1)S(1)}, bf16[2,128,8,128]{1,3,2,0:T(8,128)(2,1)S(1)}, u32[]{:S(2)}, u32[]{:S(2)}) collective-permute-start(bf16[2,128,8,128]{1,3,2,0:T(8,128)(2,1)S(1)} %pad_maximum_fusion.1), channel_id=1, source_target_pairs={{1,0},{2,1},{3,2},{4,3},{5,4},{6,5},{7,6},{8,7},{9,8},{10,9},{11,1... | collective-permute-start | bytes 1572872 | tf_op jit(solution)/shard_map/ppermute | solution.py:60
  40.0 6.9 %collective-permute-done.2 = bf16[2,128,8,128]{1,3,2,0:T(8,128)(2,1)S(1)} collective-permute-done((bf16[2,128,8,128]{1,3,2,0:T(8,128)(2,1)S(1)}, bf16[2,128,8,128]{1,3,2,0:T(8,128)(2,1)S(1)}, u32[]{:S(2)}, u32[]{:S(2)}) %collective-permute-start.2) | collective-permute-done | bytes 524320 | tf_op jit(solution)/shard_map/ppermute | solution.py:57
  46.9 3.0 %collective-permute-start.10 = (bf16[2,128,8,128]{1,3,2,0:T(8,128)(2,1)S(1)}, bf16[2,128,8,128]{1,3,2,0:T(8,128)(2,1)S(1)}, u32[]{:S(2)}, u32[]{:S(2)}) collective-permute-start(bf16[2,128,8,128]{1,3,2,0:T(8,128)(2,1)S(1)} %collective-permute-done.9), channel_id=1, source_target_pairs={{1,0},{2,1},{3,2},{4,3},{5,4},{6,5},{7,6},{8,7},{9,8},{10,9},{11,1... | collective-permute-start | bytes 1572872 | tf_op jit(solution)/shard_map/ppermute | solution.py:60
  49.9 6.9 %collective-permute-done.3 = bf16[2,128,8,128]{1,3,2,0:T(8,128)(2,1)S(1)} collective-permute-done((bf16[2,128,8,128]{1,3,2,0:T(8,128)(2,1)S(1)}, bf16[2,128,8,128]{1,3,2,0:T(8,128)(2,1)S(1)}, u32[]{:S(2)}, u32[]{:S(2)}) %collective-permute-start.3) | collective-permute-done | bytes 524320 | tf_op jit(solution)/shard_map/ppermute | solution.py:57
  56.8 2.9 %collective-permute-start.11 = (bf16[2,128,8,128]{1,3,2,0:T(8,128)(2,1)S(1)}, bf16[2,128,8,128]{1,3,2,0:T(8,128)(2,1)S(1)}, u32[]{:S(2)}, u32[]{:S(2)}) collective-permute-start(bf16[2,128,8,128]{1,3,2,0:T(8,128)(2,1)S(1)} %collective-permute-done.10), channel_id=1, source_target_pairs={{1,0},{2,1},{3,2},{4,3},{5,4},{6,5},{7,6},{8,7},{9,8},{10,9},{11,1... | collective-permute-start | bytes 1572872 | tf_op jit(solution)/shard_map/ppermute | solution.py:60
  59.7 6.8 %collective-permute-done.4 = bf16[2,128,8,128]{1,3,2,0:T(8,128)(2,1)S(1)} collective-permute-done((bf16[2,128,8,128]{1,3,2,0:T(8,128)(2,1)S(1)}, bf16[2,128,8,128]{1,3,2,0:T(8,128)(2,1)S(1)}, u32[]{:S(2)}, u32[]{:S(2)}) %collective-permute-start.4) | collective-permute-done | bytes 524320 | tf_op jit(solution)/shard_map/ppermute | solution.py:57
  66.6 2.9 %collective-permute-start.12 = (bf16[2,128,8,128]{1,3,2,0:T(8,128)(2,1)S(1)}, bf16[2,128,8,128]{1,3,2,0:T(8,128)(2,1)}, u32[]{:S(2)}, u32[]{:S(2)}) collective-permute-start(bf16[2,128,8,128]{1,3,2,0:T(8,128)(2,1)S(1)} %collective-permute-done.11), channel_id=1, source_target_pairs={{1,0},{2,1},{3,2},{4,3},{5,4},{6,5},{7,6},{8,7},{9,8},{10,9},{11,1... | collective-permute-start | bytes 1572872 | tf_op jit(solution)/shard_map/ppermute | solution.py:60
  69.5 6.8 %collective-permute-done.5 = bf16[2,128,8,128]{1,3,2,0:T(8,128)(2,1)S(1)} collective-permute-done((bf16[2,128,8,128]{1,3,2,0:T(8,128)(2,1)S(1)}, bf16[2,128,8,128]{1,3,2,0:T(8,128)(2,1)S(1)}, u32[]{:S(2)}, u32[]{:S(2)}) %collective-permute-start.5) | collective-permute-done | bytes 524320 | tf_op jit(solution)/shard_map/ppermute | solution.py:57
  76.4 3.1 %collective-permute-start.13 = (bf16[2,128,8,128]{1,3,2,0:T(8,128)(2,1)}, bf16[2,128,8,128]{1,3,2,0:T(8,128)(2,1)}, u32[]{:S(2)}, u32[]{:S(2)}) collective-permute-start(bf16[2,128,8,128]{1,3,2,0:T(8,128)(2,1)} %collective-permute-done.12), channel_id=1, source_target_pairs={{1,0},{2,1},{3,2},{4,3},{5,4},{6,5},{7,6},{8,7},{9,8},{10,9},{11,1... | collective-permute-start | bytes 1572872 | tf_op jit(solution)/shard_map/ppermute | solution.py:60
  79.5 6.8 %collective-permute-done.6 = bf16[2,128,8,128]{1,3,2,0:T(8,128)(2,1)} collective-permute-done((bf16[2,128,8,128]{1,3,2,0:T(8,128)(2,1)S(1)}, bf16[2,128,8,128]{1,3,2,0:T(8,128)(2,1)}, u32[]{:S(2)}, u32[]{:S(2)}) %collective-permute-start.6) | collective-permute-done | bytes 524320 | tf_op jit(solution)/shard_map/ppermute | solution.py:57
  86.5 3.1 %collective-permute-start.14 = (bf16[2,128,8,128]{1,3,2,0:T(8,128)(2,1)}, bf16[2,128,8,128]{1,3,2,0:T(8,128)(2,1)}, u32[]{:S(2)}, u32[]{:S(2)}) collective-permute-start(bf16[2,128,8,128]{1,3,2,0:T(8,128)(2,1)} %collective-permute-done.13), channel_id=1, source_target_pairs={{1,0},{2,1},{3,2},{4,3},{5,4},{6,5},{7,6},{8,7},{9,8},{10,9},{11,1... | collective-permute-start | bytes 1572872 | tf_op jit(solution)/shard_map/ppermute | solution.py:60
  89.6 6.8 %collective-permute-done.7 = bf16[2,128,8,128]{1,3,2,0:T(8,128)(2,1)} collective-permute-done((bf16[2,128,8,128]{1,3,2,0:T(8,128)(2,1)}, bf16[2,128,8,128]{1,3,2,0:T(8,128)(2,1)}, u32[]{:S(2)}, u32[]{:S(2)}) %collective-permute-start.7) | collective-permute-done | bytes 524320 | tf_op jit(solution)/shard_map/ppermute | solution.py:57
  96.6 1.0 copy.14
  97.7 3.0 %collective-permute-start.15 = (bf16[2,128,8,128]{1,3,2,0:T(8,128)(2,1)}, bf16[2,128,8,128]{1,3,2,0:T(8,128)(2,1)S(1)}, u32[]{:S(2)}, u32[]{:S(2)}) collective-permute-start(bf16[2,128,8,128]{1,3,2,0:T(8,128)(2,1)} %collective-permute-done.14), channel_id=1, source_target_pairs={{1,0},{2,1},{3,2},{4,3},{5,4},{6,5},{7,6},{8,7},{9,8},{10,9},{11,1... | collective-permute-start | bytes 1572872 | tf_op jit(solution)/shard_map/ppermute | solution.py:60
  100.7 5.9 %collective-permute-done.8 = bf16[2,128,8,128]{1,3,2,0:T(8,128)(2,1)} collective-permute-done((bf16[2,128,8,128]{1,3,2,0:T(8,128)(2,1)}, bf16[2,128,8,128]{1,3,2,0:T(8,128)(2,1)}, u32[]{:S(2)}, u32[]{:S(2)}) %collective-permute-start.8) | collective-permute-done | bytes 524320 | tf_op jit(solution)/shard_map/ppermute | solution.py:57
  106.6 1.9 bitcast_dynamic-update-slice_fusion.15
  108.4 1.9 bitcast_dynamic-update-slice_fusion.14
  110.3 1.9 bitcast_dynamic-update-slice_fusion.13
  112.2 1.9 bitcast_dynamic-update-slice_fusion.12
  114.2 1.9 bitcast_dynamic-update-slice_fusion.11
  116.0 1.9 bitcast_dynamic-update-slice_fusion.10
  118.0 1.9 bitcast_dynamic-update-slice_fusion.9
  122.3 0.9 bitcast_dynamic-update-slice_fusion.5
  124.1 1.9 bitcast_dynamic-update-slice_fusion.3
  126.0 1.9 bitcast_dynamic-update-slice_fusion.2
  127.8 1.9 bitcast_dynamic-update-slice_fusion.1
  129.7 0.9 bitcast_dynamic-update-slice_fusion
  130.6 8.2 %gather_fusion = bf16[16,2,128,8,128]{2,4,3,1,0:T(8,128)(2,1)} fusion(bf16[16,2,128,8,128]{2,4,3,1,0:T(8,128)(2,1)} %bitcast_dynamic-update-slice_fusion, s32[1024]{0:T(1024)S(1)} %pad_clamp_fusion), kind=kCustom, calls=%fused_computation | custom fusion | bytes 16777280 | tf_op jit(solution)/shard_map/gather | solution.py:64
  138.8 6.0 %fusion.30 = (bf16[1,16,128,8,128]{2,4,3,0,1:T(8,128)(2,1)}, bf16[1,16,128,8,128]{2,4,3,0,1:T(8,128)(2,1)}) fusion(bf16[2,16,128,8,128]{2,4,3,0,1:T(8,128)(2,1)} %bitcast.73), kind=kLoop, calls=%fused_computation.60 | loop fusion | bytes 16777216 | tf_op jit(solution)/shard_map/slice | solution.py:96
  144.8 6.5 %copy.15 = bf16[1,16,128,8,128]{4,2,1,3,0:T(8,128)(2,1)} copy(bf16[1,16,128,8,128]{2,4,3,0,1:T(8,128)(2,1)} %get-tuple-element.7) | data formatting | bytes 8388608 | tf_op jit(solution)/shard_map/slice | solution.py:96
  151.3 6.9 %copy.13 = bf16[1,16,128,8,128]{2,1,4,3,0:T(8,128)(2,1)} copy(bf16[1,16,128,8,128]{2,4,3,0,1:T(8,128)(2,1)} %get-tuple-element.8) | data formatting | bytes 8388608 | tf_op jit(solution)/shard_map/slice | solution.py:96
  158.2 7.4 %squeeze.6 = bf16[2048,8,128]{0,2,1:T(8,128)(2,1)} reshape(bf16[1,16,128,8,128]{2,1,4,3,0:T(8,128)(2,1)} %copy.13) | data formatting | bytes 8388608 | tf_op jit(solution)/shard_map/squeeze | solution.py:96
  165.5 4.9 %fusion = (f32[8,128]{1,0:T(8,128)S(1)}, f32[8,128,2048]{2,1,0:T(8,128)S(1)}) fusion(f32[8]{0:T(128)S(1)} %copy-done.13, pred[128,2048]{1,0:T(8,128)(4,1)S(1)} %iota_compare_fusion, bf16[2048,8,128]{2,0,1:T(8,128)(2,1)} %bitcast.76, f32[128,8,128]{2,0,1:T(8,128)S(1)} %copy-done.12, f32[128,8]{0,1:T(8,128)S(1)} %add_rsqrt_fusion), kind=kOutput, calls=%fused_computation.2 | convolution fusion | flops 545520640 | bytes 13377568 | tf_op jit(solution)/shard_map/jsg,isg->sji/dot_general | solution.py:98
  170.5 2.0 fusion.22
  172.5 2.7 %convolution_bitcast_fusion = f32[128,32,256]{2,0,1:T(8,128)} fusion(bf16[128,32,32]{0,2,1:T(8,128)(2,1)S(1)} %bitcast.82, bf16[32,32,256]{2,1,0:T(8,128)(2,1)S(1)} %copy-done.3), kind=kOutput, calls=%fused_computation.13 | convolution fusion | flops 67108864 | bytes 4980736 | tf_op jit(solution)/shard_map/jgc,gcu->jgu/dot_general | solution.py:117
  175.3 5.6 %copy.16 = f32[128,32,256]{0,2,1:T(8,128)} copy(f32[128,32,256]{2,0,1:T(8,128)} %convolution_bitcast_fusion) | data formatting | bytes 8388608 | tf_op jit(solution)/shard_map/jgc,gcu->jgu/transpose | solution.py:117
  180.8 9.2 %copy.17 = f32[128,4,32,64]{3,2,1,0:T(8,128)} copy(f32[128,4,32,64]{0,3,1,2:T(8,128)} %bitcast.75) | data formatting | bytes 8388608 | tf_op jit(solution)/shard_map/transpose | solution.py:122
  190.0 8.0 %reshape.153 = f32[512,2048]{1,0:T(8,128)} reshape(f32[128,4,32,64]{3,2,1,0:T(8,128)} %copy.17) | data formatting | bytes 8388608 | tf_op jit(solution)/shard_map/reshape | solution.py:123
  198.0 2.8 %multiply_reduce_fusion = f32[512]{0:T(512)S(1)} fusion(f32[512,2048]{1,0:T(8,128)} %reshape.153, bf16[512,2048]{1,0:T(8,128)(2,1)S(1)} %copy-done.1), kind=kLoop, calls=%fused_computation.8 | loop fusion | flops 4193792 | bytes 6293504 | tf_op jit(solution)/shard_map/reduce_sum | solution.py:126
  200.8 3.7 %fusion.18 = bf16[512,256]{1,0:T(8,128)(2,1)} fusion(bf16[256,2048]{1,0:T(8,128)(2,1)S(1)} %copy-done, f32[512,2048]{1,0:T(8,128)} %reshape.153, bf16[512,2048]{1,0:T(8,128)(2,1)S(1)} %copy-done.1, f32[512]{0:T(512)S(1)} %add_rsqrt_fusion.2), kind=kOutput, calls=%fused_computation.20 | convolution fusion | flops 541327360 | bytes 7604224 | tf_op jit(solution)/shard_map/dot_general | solution.py:129
  (60 shorter events, 4.2 us)
Async XLA Ops:
  0.0 200.8 %copy-start = (bf16[256,2048]{1,0:T(8,128)(2,1)S(1)}, bf16[256,2048]{1,0:T(8,128)(2,1)}, u32[]{:S(2)}) copy-start(bf16[256,2048]{1,0:T(8,128)(2,1)} %param.6) | copy-start | bytes 3145732
  0.9 5.6 %collective-permute-start = (bf16[3,2048]{1,0:T(4,128)(2,1)S(1)}, bf16[3,2048]{1,0:T(4,128)(2,1)S(1)}, u32[]{:S(2)}, u32[]{:S(2)}) collective-permute-start(bf16[3,2048]{1,0:T(4,128)(2,1)S(1)} %slice.24), channel_id=1, source_target_pairs={{0,1},{1,2},{2,3},{3,4},{4,5},{5,6},{6,7},{7,8},{8,9},{9,10},{10,1... | collective-permute-start | bytes 36872 | tf_op jit(solution)/shard_map/ppermute | solution.py:22
  22.2 14.9 %collective-permute-start.1 = (bf16[2,128,8,128]{1,3,2,0:T(8,128)(2,1)S(1)}, bf16[2,128,8,128]{1,3,2,0:T(8,128)(2,1)S(1)}, u32[]{:S(2)}, u32[]{:S(2)}) collective-permute-start(bf16[2,128,8,128]{1,3,2,0:T(8,128)(2,1)S(1)} %pad_maximum_fusion.1), channel_id=1, source_target_pairs={{0,1},{1,2},{2,3},{3,4},{4,5},{5,6},{6,7},{7,8},{8,9},{9,10},{10,1... | collective-permute-start | bytes 1572872 | tf_op jit(solution)/shard_map/ppermute | solution.py:57
  37.1 9.8 %collective-permute-start.2 = (bf16[2,128,8,128]{1,3,2,0:T(8,128)(2,1)S(1)}, bf16[2,128,8,128]{1,3,2,0:T(8,128)(2,1)S(1)}, u32[]{:S(2)}, u32[]{:S(2)}) collective-permute-start(bf16[2,128,8,128]{1,3,2,0:T(8,128)(2,1)S(1)} %collective-permute-done.1), channel_id=1, source_target_pairs={{0,1},{1,2},{2,3},{3,4},{4,5},{5,6},{6,7},{7,8},{8,9},{9,10},{10,1... | collective-permute-start | bytes 1572872 | tf_op jit(solution)/shard_map/ppermute | solution.py:57
  37.1 9.8 %collective-permute-start.9 = (bf16[2,128,8,128]{1,3,2,0:T(8,128)(2,1)S(1)}, bf16[2,128,8,128]{1,3,2,0:T(8,128)(2,1)S(1)}, u32[]{:S(2)}, u32[]{:S(2)}) collective-permute-start(bf16[2,128,8,128]{1,3,2,0:T(8,128)(2,1)S(1)} %pad_maximum_fusion.1), channel_id=1, source_target_pairs={{1,0},{2,1},{3,2},{4,3},{5,4},{6,5},{7,6},{8,7},{9,8},{10,9},{11,1... | collective-permute-start | bytes 1572872 | tf_op jit(solution)/shard_map/ppermute | solution.py:60
  46.9 9.8 %copy-start.4 = (bf16[2,128,8,128]{1,3,2,0:T(8,128)(2,1)}, bf16[2,128,8,128]{1,3,2,0:T(8,128)(2,1)S(1)}, u32[]{:S(2)}) copy-start(bf16[2,128,8,128]{1,3,2,0:T(8,128)(2,1)S(1)} %collective-permute-done.2) | copy-start | bytes 1572868
  46.9 9.8 %collective-permute-start.3 = (bf16[2,128,8,128]{1,3,2,0:T(8,128)(2,1)S(1)}, bf16[2,128,8,128]{1,3,2,0:T(8,128)(2,1)S(1)}, u32[]{:S(2)}, u32[]{:S(2)}) collective-permute-start(bf16[2,128,8,128]{1,3,2,0:T(8,128)(2,1)S(1)} %collective-permute-done.2), channel_id=1, source_target_pairs={{0,1},{1,2},{2,3},{3,4},{4,5},{5,6},{6,7},{7,8},{8,9},{9,10},{10,1... | collective-permute-start | bytes 1572872 | tf_op jit(solution)/shard_map/ppermute | solution.py:57
  46.9 9.8 %collective-permute-start.10 = (bf16[2,128,8,128]{1,3,2,0:T(8,128)(2,1)S(1)}, bf16[2,128,8,128]{1,3,2,0:T(8,128)(2,1)S(1)}, u32[]{:S(2)}, u32[]{:S(2)}) collective-permute-start(bf16[2,128,8,128]{1,3,2,0:T(8,128)(2,1)S(1)} %collective-permute-done.9), channel_id=1, source_target_pairs={{1,0},{2,1},{3,2},{4,3},{5,4},{6,5},{7,6},{8,7},{9,8},{10,9},{11,1... | collective-permute-start | bytes 1572872 | tf_op jit(solution)/shard_map/ppermute | solution.py:60
  56.7 9.8 %copy-start.7 = (bf16[2,128,8,128]{1,3,2,0:T(8,128)(2,1)}, bf16[2,128,8,128]{1,3,2,0:T(8,128)(2,1)S(1)}, u32[]{:S(2)}) copy-start(bf16[2,128,8,128]{1,3,2,0:T(8,128)(2,1)S(1)} %collective-permute-done.3) | copy-start | bytes 1572868
  56.7 9.8 %collective-permute-start.4 = (bf16[2,128,8,128]{1,3,2,0:T(8,128)(2,1)S(1)}, bf16[2,128,8,128]{1,3,2,0:T(8,128)(2,1)S(1)}, u32[]{:S(2)}, u32[]{:S(2)}) collective-permute-start(bf16[2,128,8,128]{1,3,2,0:T(8,128)(2,1)S(1)} %collective-permute-done.3), channel_id=1, source_target_pairs={{0,1},{1,2},{2,3},{3,4},{4,5},{5,6},{6,7},{7,8},{8,9},{9,10},{10,1... | collective-permute-start | bytes 1572872 | tf_op jit(solution)/shard_map/ppermute | solution.py:57
  56.7 3.0 %copy-start.5 = (bf16[2,128,8,128]{1,3,2,0:T(8,128)(2,1)}, bf16[2,128,8,128]{1,3,2,0:T(8,128)(2,1)S(1)}, u32[]{:S(2)}) copy-start(bf16[2,128,8,128]{1,3,2,0:T(8,128)(2,1)S(1)} %collective-permute-done.10) | copy-start | bytes 1572868
  56.8 9.8 %collective-permute-start.11 = (bf16[2,128,8,128]{1,3,2,0:T(8,128)(2,1)S(1)}, bf16[2,128,8,128]{1,3,2,0:T(8,128)(2,1)S(1)}, u32[]{:S(2)}, u32[]{:S(2)}) collective-permute-start(bf16[2,128,8,128]{1,3,2,0:T(8,128)(2,1)S(1)} %collective-permute-done.10), channel_id=1, source_target_pairs={{1,0},{2,1},{3,2},{4,3},{5,4},{6,5},{7,6},{8,7},{9,8},{10,9},{11,1... | collective-permute-start | bytes 1572872 | tf_op jit(solution)/shard_map/ppermute | solution.py:60
  66.5 9.8 %copy-start.10 = (bf16[2,128,8,128]{1,3,2,0:T(8,128)(2,1)}, bf16[2,128,8,128]{1,3,2,0:T(8,128)(2,1)S(1)}, u32[]{:S(2)}) copy-start(bf16[2,128,8,128]{1,3,2,0:T(8,128)(2,1)S(1)} %collective-permute-done.4) | copy-start | bytes 1572868
  66.5 9.8 %collective-permute-start.5 = (bf16[2,128,8,128]{1,3,2,0:T(8,128)(2,1)S(1)}, bf16[2,128,8,128]{1,3,2,0:T(8,128)(2,1)S(1)}, u32[]{:S(2)}, u32[]{:S(2)}) collective-permute-start(bf16[2,128,8,128]{1,3,2,0:T(8,128)(2,1)S(1)} %collective-permute-done.4), channel_id=1, source_target_pairs={{0,1},{1,2},{2,3},{3,4},{4,5},{5,6},{6,7},{7,8},{8,9},{9,10},{10,1... | collective-permute-start | bytes 1572872 | tf_op jit(solution)/shard_map/ppermute | solution.py:57
  66.6 3.0 %copy-start.8 = (bf16[2,128,8,128]{1,3,2,0:T(8,128)(2,1)}, bf16[2,128,8,128]{1,3,2,0:T(8,128)(2,1)S(1)}, u32[]{:S(2)}) copy-start(bf16[2,128,8,128]{1,3,2,0:T(8,128)(2,1)S(1)} %collective-permute-done.11) | copy-start | bytes 1572868
  66.6 9.8 %collective-permute-start.12 = (bf16[2,128,8,128]{1,3,2,0:T(8,128)(2,1)S(1)}, bf16[2,128,8,128]{1,3,2,0:T(8,128)(2,1)}, u32[]{:S(2)}, u32[]{:S(2)}) collective-permute-start(bf16[2,128,8,128]{1,3,2,0:T(8,128)(2,1)S(1)} %collective-permute-done.11), channel_id=1, source_target_pairs={{1,0},{2,1},{3,2},{4,3},{5,4},{6,5},{7,6},{8,7},{9,8},{10,9},{11,1... | collective-permute-start | bytes 1572872 | tf_op jit(solution)/shard_map/ppermute | solution.py:60
  76.4 3.1 %copy-start.11 = (bf16[2,128,8,128]{1,3,2,0:T(8,128)(2,1)}, bf16[2,128,8,128]{1,3,2,0:T(8,128)(2,1)S(1)}, u32[]{:S(2)}) copy-start(bf16[2,128,8,128]{1,3,2,0:T(8,128)(2,1)S(1)} %collective-permute-done.5) | copy-start | bytes 1572868
  76.4 9.9 %collective-permute-start.6 = (bf16[2,128,8,128]{1,3,2,0:T(8,128)(2,1)S(1)}, bf16[2,128,8,128]{1,3,2,0:T(8,128)(2,1)}, u32[]{:S(2)}, u32[]{:S(2)}) collective-permute-start(bf16[2,128,8,128]{1,3,2,0:T(8,128)(2,1)S(1)} %collective-permute-done.5), channel_id=1, source_target_pairs={{0,1},{1,2},{2,3},{3,4},{4,5},{5,6},{6,7},{7,8},{8,9},{9,10},{10,1... | collective-permute-start | bytes 1572872 | tf_op jit(solution)/shard_map/ppermute | solution.py:57
  76.4 10.1 %collective-permute-start.13 = (bf16[2,128,8,128]{1,3,2,0:T(8,128)(2,1)}, bf16[2,128,8,128]{1,3,2,0:T(8,128)(2,1)}, u32[]{:S(2)}, u32[]{:S(2)}) collective-permute-start(bf16[2,128,8,128]{1,3,2,0:T(8,128)(2,1)} %collective-permute-done.12), channel_id=1, source_target_pairs={{1,0},{2,1},{3,2},{4,3},{5,4},{6,5},{7,6},{8,7},{9,8},{10,9},{11,1... | collective-permute-start | bytes 1572872 | tf_op jit(solution)/shard_map/ppermute | solution.py:60
  86.3 10.1 %collective-permute-start.7 = (bf16[2,128,8,128]{1,3,2,0:T(8,128)(2,1)}, bf16[2,128,8,128]{1,3,2,0:T(8,128)(2,1)}, u32[]{:S(2)}, u32[]{:S(2)}) collective-permute-start(bf16[2,128,8,128]{1,3,2,0:T(8,128)(2,1)} %collective-permute-done.6), channel_id=1, source_target_pairs={{0,1},{1,2},{2,3},{3,4},{4,5},{5,6},{6,7},{7,8},{8,9},{9,10},{10,1... | collective-permute-start | bytes 1572872 | tf_op jit(solution)/shard_map/ppermute | solution.py:57
  86.5 11.2 %collective-permute-start.14 = (bf16[2,128,8,128]{1,3,2,0:T(8,128)(2,1)}, bf16[2,128,8,128]{1,3,2,0:T(8,128)(2,1)}, u32[]{:S(2)}, u32[]{:S(2)}) collective-permute-start(bf16[2,128,8,128]{1,3,2,0:T(8,128)(2,1)} %collective-permute-done.13), channel_id=1, source_target_pairs={{1,0},{2,1},{3,2},{4,3},{5,4},{6,5},{7,6},{8,7},{9,8},{10,9},{11,1... | collective-permute-start | bytes 1572872 | tf_op jit(solution)/shard_map/ppermute | solution.py:60
  96.4 10.1 %collective-permute-start.8 = (bf16[2,128,8,128]{1,3,2,0:T(8,128)(2,1)}, bf16[2,128,8,128]{1,3,2,0:T(8,128)(2,1)}, u32[]{:S(2)}, u32[]{:S(2)}) collective-permute-start(bf16[2,128,8,128]{1,3,2,0:T(8,128)(2,1)} %collective-permute-done.7), channel_id=1, source_target_pairs={{0,1},{1,2},{2,3},{3,4},{4,5},{5,6},{6,7},{7,8},{8,9},{9,10},{10,1... | collective-permute-start | bytes 1572872 | tf_op jit(solution)/shard_map/ppermute | solution.py:57
  97.6 24.7 %copy-start.6 = (bf16[2,128,8,128]{1,3,2,0:T(8,128)(2,1)S(1)}, bf16[2,128,8,128]{1,3,2,0:T(8,128)(2,1)}, u32[]{:S(2)}) copy-start(bf16[2,128,8,128]{1,3,2,0:T(8,128)(2,1)} %copy-done.5) | copy-start | bytes 1572868
  97.7 25.6 %copy-start.9 = (bf16[2,128,8,128]{1,3,2,0:T(8,128)(2,1)S(1)}, bf16[2,128,8,128]{1,3,2,0:T(8,128)(2,1)}, u32[]{:S(2)}) copy-start(bf16[2,128,8,128]{1,3,2,0:T(8,128)(2,1)} %copy-done.8) | copy-start | bytes 1572868
  97.7 32.0 %collective-permute-start.15 = (bf16[2,128,8,128]{1,3,2,0:T(8,128)(2,1)}, bf16[2,128,8,128]{1,3,2,0:T(8,128)(2,1)S(1)}, u32[]{:S(2)}, u32[]{:S(2)}) collective-permute-start(bf16[2,128,8,128]{1,3,2,0:T(8,128)(2,1)} %collective-permute-done.14), channel_id=1, source_target_pairs={{1,0},{2,1},{3,2},{4,3},{5,4},{6,5},{7,6},{8,7},{9,8},{10,9},{11,1... | collective-permute-start | bytes 1572872 | tf_op jit(solution)/shard_map/ppermute | solution.py:60
  151.3 14.3 %copy-start.12 = (f32[128,8,128]{2,0,1:T(8,128)S(1)}, f32[128,8,128]{2,0,1:T(8,128)}, u32[]{:S(2)}) copy-start(f32[128,8,128]{2,0,1:T(8,128)} %copy.14) | copy-start | bytes 1572868
  151.3 14.3 %copy-start.13 = (f32[8]{0:T(128)S(1)}, f32[8]{0:T(128)}, u32[]{:S(2)}) copy-start(f32[8]{0:T(128)} %param.8) | copy-start | bytes 100
  165.5 4.9 %copy-start.2 = (bf16[2048,8,128]{0,2,1:T(8,128)(2,1)S(1)}, bf16[2048,8,128]{0,2,1:T(8,128)(2,1)}, u32[]{:S(2)}) copy-start(bf16[2048,8,128]{0,2,1:T(8,128)(2,1)} %squeeze.6) | copy-start | bytes 12582916
  170.5 2.1 %copy-start.3 = (bf16[32,32,256]{2,1,0:T(8,128)(2,1)S(1)}, bf16[32,32,256]{2,1,0:T(8,128)(2,1)}, u32[]{:S(2)}) copy-start(bf16[32,32,256]{2,1,0:T(8,128)(2,1)} %param.9) | copy-start | bytes 1572868
  190.0 8.0 %copy-start.1 = (bf16[512,2048]{1,0:T(8,128)(2,1)S(1)}, bf16[512,2048]{1,0:T(8,128)(2,1)}, u32[]{:S(2)}) copy-start(bf16[512,2048]{1,0:T(8,128)(2,1)} %param.5) | copy-start | bytes 6291460
